TPU v7x, 32 devices: a whole 2x2x4 slice. The times are simulated.
32 devices in a mesh: group: 2 (over x), sec: 16 (over z, y, core).
Axes of the slice: x: 2, y: 2, z: 4, core: 2. Of those that a mesh axis runs over, the one named last changes fastest.
Arguments:
- patches: bfloat16 [32, 128, 128, 128], P(('group', 'sec')), parts along dimension 0, may hold values from -24 to 24
- pair_list: int32 [32, 64], P(('group', 'sec')), parts along dimension 0, may hold values from 0 to 127, as said below
- pair_count: int32 [32], P(('group', 'sec')), parts along dimension 0, may hold values from 0 to 64, as said below
- tissue: int32 [32, 128], P(('group', 'sec')), parts along dimension 0, may hold values 0 or 1
Outputs:
- pair_flow: float32 [32, 2, 64], P(('group', 'sec')), parts along dimension 0
- positions: float32 [32, 2, 128], P(('group', 'sec')), parts along dimension 0
There are 2 independent parts, one for each index of `group`. A program takes and returns all parts, laid end to end along the dimension named above; each array names one. Nothing has to cross between parts.
Inputs may be any that keep to these rules, and one draw needn't show every extreme that they name: `pair_list`: the first pair_count[s] entries of row s are distinct patch indices; the other entries are 0. `pair_count`: some section other than the last has exactly 64 live slots; the last section has 0.
All inputs are finite; a program needn't handle non-finite values. No bound on the sum of `tissue` on one device may be relied on, other than what follows from the above.
Results may differ from a plain program's by a relative error of at most 0.0029.
Values may be sent and summed in bfloat16 or wider, within the bound.
A program may use at most 64 MiB of HBM per device.

v0:
```python
import functools

import jax
import jax.numpy as jnp
import numpy as np
from jax import lax
from jax.experimental import pallas as pl
from jax.experimental.pallas import tpu as pltpu
from jax.sharding import PartitionSpec as P

GR = 8
SPRING = 0.25
STEP = 0.15
CHUNK = 8
HALO = 3
MESH = pl.DeviceIdType.MESH
F32 = jnp.float32
BF16 = jnp.bfloat16


def dft_tables(length):
    index = np.arange(length)
    angle = (index[:, None] * index[None, :] % length) * (2.0 * np.pi / length)
    c = np.cos(angle).astype(np.float32)
    s = np.sin(angle).astype(np.float32)
    right = np.concatenate([c, s], axis=1)
    left = np.block([[c, -s], [-s, -c]])
    inner = np.block([[c, s], [-s, c]])
    last = np.concatenate([c, -s], axis=1)
    return tuple(jnp.asarray(t.astype(jnp.bfloat16)) for t in (right, left, inner, last))


def dot(a, b):
    return jnp.dot(a, b, preferred_element_type=F32)


def dot_nt(a, b):
    return lax.dot_general(a, b, (((1,), (1,)), ((), ())), preferred_element_type=F32)


def split3(x):
    top = x.astype(BF16)
    rest = x - top.astype(F32)
    mid = rest.astype(BF16)
    return top, mid, (rest - mid.astype(F32)).astype(BF16)


def stacked(both, a, b, side):
    ra = both[a * side : (a + 1) * side]
    rb = both[b * side : (b + 1) * side]
    top = jnp.concatenate([ra[:, :side], rb[:, :side]], axis=1)
    low = jnp.concatenate([ra[:, side:], rb[:, side:]], axis=1)
    return jnp.concatenate([top, low], axis=0)


def spectra(images, right, left):
    side = images[0].shape[0]
    rows = jnp.concatenate(images, axis=0)
    both = dot(rows, right).astype(BF16)
    return [dot(left, stacked(both, 2 * i, 2 * i + 1, side)) for i in range(len(images) // 2)]


def lane_roll(x, shift):
    return pltpu.roll(x, shift % x.shape[-1], x.ndim - 1)


def up_chunks(pair, n, chunks):
    return chunks * ((pair + 1) // 2) // (n // 2)


def exchange(
    n,
    right_any,
    left_any,
    inner_any,
    last_any,
    list_any,
    count_s,
    tissue_any,
    patches_any,
    out_ref,
    patches,
    right_ref,
    left_ref,
    inner_ref,
    last_ref,
    list_v,
    list_s,
    tissue_v,
    note,
    far_note,
    far_s,
    outgoing,
    incoming,
    own_spec,
    peak_ref,
    mass_ref,
    moment_ref,
    packet,
    halo,
    load_sems,
    smem_sem,
    list_sems,
    send_sems,
    recv_sems,
    halo_send,
    halo_recv,
):
    me = lax.axis_index("sec")
    total, side, _ = patches.shape
    slots = list_v.shape[1]
    chunks = slots // CHUNK
    offsets = [d for d in range(-HALO, HALO + 1) if d != 0]

    loads = [
        pltpu.make_async_copy(source, target, load_sems.at[i])
        for i, (source, target) in enumerate(
            (
                (list_any, list_v),
                (list_any, list_s),
                (patches_any.at[0], patches),
                (right_any, right_ref),
                (left_any, left_ref),
                (inner_any, inner_ref),
                (last_any, last_ref),
                (tissue_any, tissue_v),
            )
        )
    ]
    for load in loads:
        load.start()

    halo[...] = jnp.zeros_like(halo)
    far_note[...] = jnp.zeros_like(far_note)

    barrier = pltpu.get_barrier_semaphore()
    for d in offsets:

        @pl.when((me + d >= 0) & (me + d < n))
        def _():
            pl.semaphore_signal(barrier, inc=1, device_id={"sec": me + d}, device_id_type=MESH)

    peak_ref[...] = jnp.zeros_like(peak_ref)
    mass_ref[...] = jnp.ones_like(mass_ref)
    moment_ref[...] = jnp.zeros_like(moment_ref)
    for load in loads[:2]:
        load.wait()
    count = count_s[0]
    note[...] = jnp.concatenate([list_v[...], jnp.full((1, slots), count, jnp.int32)], axis=0)

    has_up = jnp.minimum(n - 1 - me, 1)
    has_down = jnp.minimum(me, 1)
    my_up = up_chunks(me, n, chunks)
    far_up = up_chunks(me - 1, n, chunks)

    pl.semaphore_wait(barrier, jnp.minimum(me, HALO) + jnp.minimum(n - 1 - me, HALO))

    list_copy = pltpu.make_async_remote_copy(
        src_ref=note,
        dst_ref=far_note,
        send_sem=list_sems.at[0],
        recv_sem=list_sems.at[1],
        device_id={"sec": me + 1},
        device_id_type=MESH,
    )

    @pl.when(me < n - 1)
    def _():
        list_copy.start()

    loads[2].wait()

    def patch_copy(q, to):
        return pltpu.make_async_remote_copy(
            src_ref=outgoing.at[pl.ds(q * CHUNK, CHUNK)],
            dst_ref=incoming.at[pl.ds(q * CHUNK, CHUNK)],
            send_sem=send_sems.at[q],
            recv_sem=recv_sems.at[q],
            device_id={"sec": to},
            device_id_type=MESH,
        )

    def send_up(c, carry):
        for j in range(CHUNK):
            outgoing[c * CHUNK + j] = patches[list_s[0, c * CHUNK + j]]
        patch_copy(c, me + 1).start()
        return carry

    lax.fori_loop(0, has_up * my_up, send_up, 0)
    for load in loads[3:]:
        load.wait()

    def own_group(q, carry):
        images = []
        for j in range(CHUNK):
            far = far_s[0, jnp.minimum(q, chunks - 1) * CHUNK + j]
            near = list_s[0, jnp.maximum(q - chunks, 0) * CHUNK + j]
            images.append(patches[jnp.where(q < chunks, far, near)])
        for i, spec in enumerate(spectra(images, right_ref[...], left_ref[...])):
            own_spec[q * (CHUNK // 2) + i] = spec.astype(BF16)
        return carry

    @pl.when(me > 0)
    def _():
        list_copy.wait_recv()

    to_smem = pltpu.make_async_copy(far_note, far_s, smem_sem)
    to_smem.start()
    to_smem.wait()

    def send_down(c, carry):
        for j in range(CHUNK):
            outgoing[slots + c * CHUNK + j] = patches[far_s[0, c * CHUNK + j]]
        patch_copy(chunks + c, me - 1).start()
        return carry

    lax.fori_loop(far_up, far_up + has_down * (chunks - far_up), send_down, 0)
    lax.fori_loop(chunks + my_up, chunks + my_up + has_up * (chunks - my_up), own_group, 0)
    lax.fori_loop(0, has_down * far_up, own_group, 0)

    half = side // 2
    row = lax.broadcasted_iota(jnp.int32, (side, 1), 0)
    row_lag = ((row + half) % side - half).astype(F32)
    scale = 64.0 / float(side * side * side * side)

    def match_group(t, carry):
        start_a, count_a, start_b = carry
        q = jnp.where(t < count_a, start_a + t, start_b + t - count_a)
        patch_copy(q, me).wait_recv()
        sign = jnp.where(q < chunks, -1.0, 1.0).astype(F32)
        images = [incoming[q * CHUNK + j] for j in range(CHUNK)]
        crosses = []
        for i, spec in enumerate(spectra(images, right_ref[...], left_ref[...])):
            ar = spec[:side].astype(BF16).astype(F32)
            ai = spec[side:].astype(BF16).astype(F32)
            own = own_spec[q * (CHUNK // 2) + i].astype(F32)
            br, bi = own[:side], own[side:]
            cr = (br * ar + bi * ai).astype(BF16)
            ci = ((br * ai - bi * ar) * sign).astype(BF16)
            crosses.append(jnp.concatenate([cr[:, :side], ci[:, :side]], axis=1))
            crosses.append(jnp.concatenate([cr[:, side:], ci[:, side:]], axis=1))
        inner = dot(jnp.concatenate(crosses, axis=0), inner_ref[...]).astype(BF16)
        peaks, masses, moments = [], [], []
        for i in range(CHUNK // 2):
            scores = dot(last_ref[...], stacked(inner, 2 * i, 2 * i + 1, side)) * scale
            peak = jnp.max(scores, axis=0, keepdims=True)
            e = jnp.exp(scores - peak)
            mass = jnp.sum(e, axis=0, keepdims=True)
            moment = jnp.sum(e * row_lag, axis=0, keepdims=True)
            for parts, value in ((peaks, peak), (masses, mass), (moments, moment)):
                parts.append(value[:, :side])
                parts.append(value[:, side:])
        at = pl.ds(pl.multiple_of(q * CHUNK, CHUNK), CHUNK)
        peak_ref[at, :] = jnp.concatenate(peaks, axis=0)
        mass_ref[at, :] = jnp.concatenate(masses, axis=0)
        moment_ref[at, :] = jnp.concatenate(moments, axis=0)
        return carry

    n_far = has_down * far_up
    n_near = has_up * (chunks - my_up)
    odd = me % 2
    start_a = (1 - odd) * (chunks + my_up)
    start_b = odd * (chunks + my_up)
    count_a = odd * n_far + (1 - odd) * n_near
    lax.fori_loop(0, n_far + n_near, match_group, (start_a, count_a, start_b))

    peak = peak_ref[...]
    weight = jnp.exp(peak - jnp.max(peak, axis=1, keepdims=True))
    mass = mass_ref[...] * weight
    moment = moment_ref[...] * weight
    col = lax.broadcasted_iota(jnp.int32, (8, side), 1)
    sub = lax.broadcasted_iota(jnp.int32, (8, side), 0)
    col_lag = ((col + half) % side - half).astype(F32)
    axes = jnp.where(sub == 0, 1.0, jnp.where(sub == 1, col_lag, 0.0))
    thirds = jnp.concatenate(split3(jnp.concatenate([mass, moment], axis=0)), axis=0)
    triple = dot_nt(axes.astype(BF16), thirds)
    span = 4 * slots
    joined = triple[:, 0:span] + triple[:, span : 2 * span] + triple[:, 2 * span :]
    sums, rows_num = joined[:, 0 : 2 * slots], joined[:, 2 * slots :]
    mass_all = sums[0:1]
    place = lax.broadcasted_iota(jnp.int32, (1, 2 * slots), 1)
    is_far = place < slots
    far = far_note[...]
    counts = jnp.concatenate([far[1:2], jnp.full((1, slots), count, jnp.int32)], axis=1)
    lists = jnp.concatenate([far[0:1], list_v[...]], axis=1)
    slot = jnp.where(is_far, place, place - slots)
    first = jnp.where(is_far, 0, (chunks - n_near) * CHUNK)
    stop = jnp.minimum(jnp.where(is_far, n_far * CHUNK, slots), counts)
    live = (slot >= first) & (slot < stop)
    flow_rows = jnp.where(live, rows_num[0:1] / mass_all, 0.0)
    flow_cols = jnp.where(live, sums[1:2] / mass_all, 0.0)
    which = lax.broadcasted_iota(jnp.int32, (total, 2 * slots), 0)
    onehot = (which == lists).astype(F32).astype(BF16)
    one_pair = jnp.concatenate(
        [flow_rows, flow_cols, live.astype(F32), jnp.zeros((5, 2 * slots), F32)], axis=0
    )
    both = jnp.concatenate(
        [jnp.where(is_far, one_pair, 0.0), jnp.where(is_far, 0.0, one_pair)], axis=0
    )
    triple = dot_nt(jnp.concatenate(split3(both), axis=0), onehot)
    field = triple[0:16] + triple[16:32] + triple[32:48]
    packet[0:3] = field[0:3]
    packet[3:4] = tissue_v[...].astype(F32)
    packet[4:8] = field[4:8]
    packet[8:16] = field[8:16]
    packet[4:5, 0 : 2 * slots] = flow_rows
    packet[5:6, 0 : 2 * slots] = flow_cols

    def halo_copy(d):
        return pltpu.make_async_remote_copy(
            src_ref=packet,
            dst_ref=halo.at[HALO - d],
            send_sem=halo_send.at[HALO - d],
            recv_sem=halo_recv.at[HALO - d],
            device_id={"sec": me + d},
            device_id_type=MESH,
        )

    for d in offsets:

        @pl.when((me + d >= 0) & (me + d < n))
        def _():
            halo_copy(d).start()

    @pl.when(me < n - 1)
    def _():
        list_copy.wait_send()

    def drain_up(c, carry):
        patch_copy(c, me + 1).wait_send()
        return carry

    lax.fori_loop(0, has_up * my_up, drain_up, 0)

    def drain_down(c, carry):
        patch_copy(chunks + c, me - 1).wait_send()
        return carry

    lax.fori_loop(far_up, far_up + has_down * (chunks - far_up), drain_down, 0)
    for d in offsets:

        @pl.when((me - d >= 0) & (me - d < n))
        def _():
            halo_copy(d).wait_recv()

    for d in offsets:
        out_ref[HALO + d] = halo[HALO + d]
    out_ref[HALO] = packet[...]
    for d in offsets:

        @pl.when((me + d >= 0) & (me + d < n))
        def _():
            halo_copy(d).wait_send()


def relax(halo, flow_ref, pos_ref):
    total = halo.shape[-1]
    slots = flow_ref.shape[-1]
    near, above = halo[HALO], halo[HALO + 1]
    flow_ref[0] = near[4:6, slots : 2 * slots] + above[4:6, 0:slots]
    fields = {d: halo[HALO + d][8:16] + halo[HALO + d + 1][0:8] for d in range(-HALO, HALO)}
    links = {d: jnp.broadcast_to(f[2:3], f.shape) for d, f in fields.items()}
    lane = lax.broadcasted_iota(jnp.int32, (8, total), 1)
    width = total // GR
    has_right = (lane % width) != width - 1
    has_below = lane < total - width

    def springs(d):
        tissue = jnp.broadcast_to(halo[HALO + d][3:4], (8, total))
        stiff = SPRING * (1.0 + 2.0 * tissue)
        across = jnp.where(has_right, 0.5 * (stiff + lane_roll(stiff, -1)), 0.0)
        along = jnp.where(has_below, 0.5 * (stiff + lane_roll(stiff, -width)), 0.0)
        return across, along

    def plane(u, spring):
        across, along = spring
        a = across * (lane_roll(u, -1) - u)
        b = along * (lane_roll(u, -width) - u)
        return (lane_roll(a, 1) - a) + (lane_roll(b, width) - b)

    spring = {d: springs(d) for d in (-1, 0, 1)}
    pull = {d: links[d] * fields[d] for d in fields}
    u1 = {d: -STEP * (pull[d] - pull[d - 1]) for d in range(-2, 3)}

    def relaxed(u, d):
        gap_here = u[d + 1] - u[d] - fields[d]
        gap_below = u[d] - u[d - 1] - fields[d - 1]
        force = plane(u[d], spring[d]) - links[d] * gap_here + links[d - 1] * gap_below
        return u[d] - STEP * force

    u2 = {d: relaxed(u1, d) for d in (-1, 0, 1)}
    pos_ref[0] = relaxed(u2, 0)[0:2]


def on_device(n, patches, pair_list, pair_count, tissue):
    _, total, side, _ = patches.shape
    slots = pair_list.shape[1]
    chunks = slots // CHUNK
    vmem = pl.BlockSpec(memory_space=pltpu.VMEM)
    any_space = pl.BlockSpec(memory_space=pl.ANY)
    dma = pltpu.SemaphoreType.DMA
    halo = pl.pallas_call(
        functools.partial(exchange, n),
        out_shape=jax.ShapeDtypeStruct((2 * HALO + 1, 16, total), F32),
        in_specs=[any_space] * 5 + [pl.BlockSpec(memory_space=pltpu.SMEM)] + [any_space] * 2,
        out_specs=vmem,
        scratch_shapes=[
            pltpu.VMEM((total, side, side), BF16),
            pltpu.VMEM((side, 2 * side), BF16),
            pltpu.VMEM((2 * side, 2 * side), BF16),
            pltpu.VMEM((2 * side, 2 * side), BF16),
            pltpu.VMEM((side, 2 * side), BF16),
            pltpu.VMEM((1, slots), jnp.int32),
            pltpu.SMEM((1, slots), jnp.int32),
            pltpu.VMEM((1, total), jnp.int32),
            pltpu.VMEM((2, slots), jnp.int32),
            pltpu.VMEM((2, slots), jnp.int32),
            pltpu.SMEM((2, slots), jnp.int32),
            pltpu.VMEM((2 * slots, side, side), BF16),
            pltpu.VMEM((2 * slots, side, side), BF16),
            pltpu.VMEM((slots, 2 * side, 2 * side), BF16),
            pltpu.VMEM((2 * slots, side), F32),
            pltpu.VMEM((2 * slots, side), F32),
            pltpu.VMEM((2 * slots, side), F32),
            pltpu.VMEM((16, total), F32),
            pltpu.VMEM((2 * HALO + 1, 16, total), F32),
            dma((8,)),
            dma,
            dma((2,)),
            dma((2 * chunks,)),
            dma((2 * chunks,)),
            dma((2 * HALO + 1,)),
            dma((2 * HALO + 1,)),
        ],
        compiler_params=pltpu.CompilerParams(
            collective_id=0, has_side_effects=True, vmem_limit_bytes=64_000_000
        ),
        name="exchange",
    )(*dft_tables(side), pair_list, pair_count, tissue, patches)
    return pl.pallas_call(
        relax,
        out_shape=(
            jax.ShapeDtypeStruct((1, 2, slots), F32),
            jax.ShapeDtypeStruct((1, 2, total), F32),
        ),
        in_specs=[vmem],
        out_specs=(vmem, vmem),
        name="relax",
    )(halo)


def solution(mesh):
    return jax.shard_map(
        functools.partial(on_device, mesh.shape["sec"]),
        mesh=mesh,
        in_specs=(
            P(("group", "sec"), None, None, None),
            P(("group", "sec"), None),
            P(("group", "sec")),
            P(("group", "sec"), None),
        ),
        out_specs=(P(("group", "sec"), None, None), P(("group", "sec"), None, None)),
        check_vma=False,
    )
```

profile of v0, /device:TPU:0, one launch (start us, length us, event | category | flops | bytes accessed | tf_op | source)
XLA Modules:
  0.0 33.9 jit_solution(3844641943604886923)
XLA Ops:
  1.3 31.0 %exchange.1.halo = f32[7,16,128]{2,1,0:T(8,128)} custom-call(bf16[128,256]{1,0:T(8,128)(2,1)} %constant.8.clone.right_any, bf16[256,256]{1,0:T(8,128)(2,1)} %constant.9.clone.left_any, bf16[256,256]{1,0:T(8,128)(2,1)} %constant.10.clone.inner_any, bf16[128,256]{1,0:T(8,128)(2,1)} %constant.11.clone.last_any, s32[1,64]{1,0:T(1,128)} %list_any.1, ...), custom_call_target="tpu_custom_call" | custom-call | tf_op jit(solution)/shard_map/exchange/pallas_call | solution.py:402
  32.2 1.7 %relax.1 = (f32[1,2,64]{2,1,0:T(2,128)}, f32[1,2,128]{2,1,0:T(2,128)}) custom-call(f32[7,16,128]{2,1,0:T(8,128)} %exchange.1.halo), custom_call_target="tpu_custom_call" | custom-call | tf_op jit(solution)/shard_map/relax/pallas_call | solution.py:440
where the time goes:
time: 34.1 us; the launch traced here: 33.9 us
  Pallas kernels  32.6 us (96%)
  between operations  1.28 us (4%)
    pallas_call x1, Pallas kernels, on_device(): pl.pallas_call(functools.partial(exchange, n), out_shape=jax.ShapeDtypeSt...  31 us
    pallas_call x1, Pallas kernels, on_device(): pl.pallas_call(relax, out_shape=(jax.ShapeDtypeStruct((1, 2, slots), F32)...  1.68 us

commit v1 on v0

--- a/solution.py
+++ b/solution.py
@@ -12,6 +12,8 @@
 SPRING = 0.25
 STEP = 0.15
 CHUNK = 8
+PIECE = 2
+LOADS = 4
 HALO = 3
 MESH = pl.DeviceIdType.MESH
 F32 = jnp.float32
@@ -27,7 +29,8 @@
     left = np.block([[c, -s], [-s, -c]])
     inner = np.block([[c, s], [-s, c]])
     last = np.concatenate([c, -s], axis=1)
-    return tuple(jnp.asarray(t.astype(jnp.bfloat16)) for t in (right, left, inner, last))
+    tables = np.concatenate([right, left, inner, last], axis=0)
+    return jnp.asarray(tables.astype(jnp.bfloat16))
 
 
 def dot(a, b):
@@ -64,26 +67,24 @@
     return pltpu.roll(x, shift % x.shape[-1], x.ndim - 1)
 
 
+def single(pair):
+    return pair % 2
+
+
 def up_chunks(pair, n, chunks):
     return chunks * ((pair + 1) // 2) // (n // 2)
 
 
 def exchange(
     n,
-    right_any,
-    left_any,
-    inner_any,
-    last_any,
+    tables_any,
     list_any,
     count_s,
     tissue_any,
     patches_any,
     out_ref,
     patches,
-    right_ref,
-    left_ref,
-    inner_ref,
-    last_ref,
+    tables,
     list_v,
     list_s,
     tissue_v,
@@ -116,19 +117,22 @@
         pltpu.make_async_copy(source, target, load_sems.at[i])
         for i, (source, target) in enumerate(
             (
+                (list_any, list_s),
                 (list_any, list_v),
-                (list_any, list_s),
                 (patches_any.at[0], patches),
-                (right_any, right_ref),
-                (left_any, left_ref),
-                (inner_any, inner_ref),
-                (last_any, last_ref),
+                (tables_any, tables),
                 (tissue_any, tissue_v),
             )
         )
     ]
-    for load in loads:
-        load.start()
+    loads[0].start()
+    loads[1].start()
+    part = total // LOADS
+    for i in range(LOADS):
+        rows = pl.ds(i * part, part)
+        pltpu.make_async_copy(patches_any.at[0, rows], patches.at[rows], load_sems.at[2]).start()
+    loads[3].start()
+    loads[4].start()
 
     halo[...] = jnp.zeros_like(halo)
     far_note[...] = jnp.zeros_like(far_note)
@@ -143,8 +147,8 @@
     peak_ref[...] = jnp.zeros_like(peak_ref)
     mass_ref[...] = jnp.ones_like(mass_ref)
     moment_ref[...] = jnp.zeros_like(moment_ref)
-    for load in loads[:2]:
-        load.wait()
+    loads[0].wait()
+    loads[1].wait()
     count = count_s[0]
     note[...] = jnp.concatenate([list_v[...], jnp.full((1, slots), count, jnp.int32)], axis=0)
 
@@ -152,6 +156,8 @@
     has_down = jnp.minimum(me, 1)
     my_up = up_chunks(me, n, chunks)
     far_up = up_chunks(me - 1, n, chunks)
+    my_half = has_up * single(me)
+    far_half = has_down * single(me - 1)
 
     pl.semaphore_wait(barrier, jnp.minimum(me, HALO) + jnp.minimum(n - 1 - me, HALO))
 
@@ -180,15 +186,37 @@
             device_id_type=MESH,
         )
 
+    def piece_copy(q, first, size, to):
+        at = pl.ds(q * CHUNK + first, size)
+        return pltpu.make_async_remote_copy(
+            src_ref=outgoing.at[at],
+            dst_ref=incoming.at[at],
+            send_sem=send_sems.at[q],
+            recv_sem=recv_sems.at[q],
+            device_id={"sec": to},
+            device_id_type=MESH,
+        )
+
+    def gather(source, q, c, first, count):
+        for j in range(first, first + count):
+            outgoing[q * CHUNK + j] = patches[source[0, c * CHUNK + j]]
+
     def send_up(c, carry):
-        for j in range(CHUNK):
-            outgoing[c * CHUNK + j] = patches[list_s[0, c * CHUNK + j]]
+        gather(list_s, c, c, 0, CHUNK)
         patch_copy(c, me + 1).start()
         return carry
 
     lax.fori_loop(0, has_up * my_up, send_up, 0)
-    for load in loads[3:]:
-        load.wait()
+
+    @pl.when(my_half > 0)
+    def _():
+        gather(list_s, my_up, my_up, 0, PIECE)
+        piece_copy(my_up, 0, PIECE, me + 1).start()
+
+    right_ref = tables.at[0:side]
+    left_ref = tables.at[side : 3 * side]
+    inner_ref = tables.at[3 * side : 5 * side]
+    last_ref = tables.at[5 * side : 6 * side]
 
     def own_group(q, carry):
         images = []
@@ -208,15 +236,23 @@
     to_smem.start()
     to_smem.wait()
 
+    @pl.when(far_half > 0)
+    def _():
+        gather(far_s, chunks + far_up, far_up, PIECE, CHUNK - PIECE)
+        piece_copy(chunks + far_up, PIECE, CHUNK - PIECE, me - 1).start()
+
+    down_from = far_up + far_half
+
     def send_down(c, carry):
-        for j in range(CHUNK):
-            outgoing[slots + c * CHUNK + j] = patches[far_s[0, c * CHUNK + j]]
+        gather(far_s, chunks + c, c, 0, CHUNK)
         patch_copy(chunks + c, me - 1).start()
         return carry
 
-    lax.fori_loop(far_up, far_up + has_down * (chunks - far_up), send_down, 0)
+    lax.fori_loop(down_from, down_from + has_down * (chunks - down_from), send_down, 0)
+    for load in loads[3:]:
+        load.wait()
     lax.fori_loop(chunks + my_up, chunks + my_up + has_up * (chunks - my_up), own_group, 0)
-    lax.fori_loop(0, has_down * far_up, own_group, 0)
+    lax.fori_loop(0, has_down * far_up + far_half, own_group, 0)
 
     half = side // 2
     row = lax.broadcasted_iota(jnp.int32, (side, 1), 0)
@@ -226,7 +262,21 @@
     def match_group(t, carry):
         start_a, count_a, start_b = carry
         q = jnp.where(t < count_a, start_a + t, start_b + t - count_a)
-        patch_copy(q, me).wait_recv()
+        is_far_half = (q == far_up) & (far_half > 0)
+        is_my_half = (q == chunks + my_up) & (my_half > 0)
+
+        @pl.when(is_far_half)
+        def _():
+            piece_copy(q, 0, PIECE, me).wait_recv()
+
+        @pl.when(is_my_half)
+        def _():
+            piece_copy(q, PIECE, CHUNK - PIECE, me).wait_recv()
+
+        @pl.when(jnp.logical_not(is_far_half | is_my_half))
+        def _():
+            patch_copy(q, me).wait_recv()
+
         sign = jnp.where(q < chunks, -1.0, 1.0).astype(F32)
         images = [incoming[q * CHUNK + j] for j in range(CHUNK)]
         crosses = []
@@ -256,7 +306,7 @@
         moment_ref[at, :] = jnp.concatenate(moments, axis=0)
         return carry
 
-    n_far = has_down * far_up
+    n_far = has_down * far_up + far_half
     n_near = has_up * (chunks - my_up)
     odd = me % 2
     start_a = (1 - odd) * (chunks + my_up)
@@ -284,8 +334,8 @@
     counts = jnp.concatenate([far[1:2], jnp.full((1, slots), count, jnp.int32)], axis=1)
     lists = jnp.concatenate([far[0:1], list_v[...]], axis=1)
     slot = jnp.where(is_far, place, place - slots)
-    first = jnp.where(is_far, 0, (chunks - n_near) * CHUNK)
-    stop = jnp.minimum(jnp.where(is_far, n_far * CHUNK, slots), counts)
+    first = jnp.where(is_far, 0, (chunks - n_near) * CHUNK + my_half * PIECE)
+    stop = jnp.minimum(jnp.where(is_far, n_far * CHUNK - far_half * (CHUNK - PIECE), slots), counts)
     live = (slot >= first) & (slot < stop)
     flow_rows = jnp.where(live, rows_num[0:1] / mass_all, 0.0)
     flow_cols = jnp.where(live, sums[1:2] / mass_all, 0.0)
@@ -332,32 +382,39 @@
 
     lax.fori_loop(0, has_up * my_up, drain_up, 0)
 
+    @pl.when(my_half > 0)
+    def _():
+        piece_copy(my_up, 0, PIECE, me + 1).wait_send()
+
     def drain_down(c, carry):
         patch_copy(chunks + c, me - 1).wait_send()
         return carry
 
-    lax.fori_loop(far_up, far_up + has_down * (chunks - far_up), drain_down, 0)
+    lax.fori_loop(down_from, down_from + has_down * (chunks - down_from), drain_down, 0)
+
+    @pl.when(far_half > 0)
+    def _():
+        piece_copy(chunks + far_up, PIECE, CHUNK - PIECE, me - 1).wait_send()
+
     for d in offsets:
 
         @pl.when((me - d >= 0) & (me - d < n))
         def _():
             halo_copy(d).wait_recv()
 
+    halo[HALO] = packet[...]
+    relax(slots, halo, out_ref)
     for d in offsets:
-        out_ref[HALO + d] = halo[HALO + d]
-    out_ref[HALO] = packet[...]
-    for d in offsets:
 
         @pl.when((me + d >= 0) & (me + d < n))
         def _():
             halo_copy(d).wait_send()
 
 
-def relax(halo, flow_ref, pos_ref):
+def relax(slots, halo, out_ref):
     total = halo.shape[-1]
-    slots = flow_ref.shape[-1]
     near, above = halo[HALO], halo[HALO + 1]
-    flow_ref[0] = near[4:6, slots : 2 * slots] + above[4:6, 0:slots]
+    out_ref[2:4, 0:slots] = near[4:6, slots : 2 * slots] + above[4:6, 0:slots]
     fields = {d: halo[HALO + d][8:16] + halo[HALO + d + 1][0:8] for d in range(-HALO, HALO)}
     links = {d: jnp.broadcast_to(f[2:3], f.shape) for d, f in fields.items()}
     lane = lax.broadcasted_iota(jnp.int32, (8, total), 1)
@@ -389,7 +446,12 @@
         return u[d] - STEP * force
 
     u2 = {d: relaxed(u1, d) for d in (-1, 0, 1)}
-    pos_ref[0] = relaxed(u2, 0)[0:2]
+    out_ref[0:2] = relaxed(u2, 0)[0:2]
+
+
+def unpack(both, flow_ref, pos_ref):
+    flow_ref[0] = both[2:4, 0 : flow_ref.shape[-1]]
+    pos_ref[0] = both[0:2]
 
 
 def on_device(n, patches, pair_list, pair_count, tissue):
@@ -399,17 +461,14 @@
     vmem = pl.BlockSpec(memory_space=pltpu.VMEM)
     any_space = pl.BlockSpec(memory_space=pl.ANY)
     dma = pltpu.SemaphoreType.DMA
-    halo = pl.pallas_call(
+    both = pl.pallas_call(
         functools.partial(exchange, n),
-        out_shape=jax.ShapeDtypeStruct((2 * HALO + 1, 16, total), F32),
-        in_specs=[any_space] * 5 + [pl.BlockSpec(memory_space=pltpu.SMEM)] + [any_space] * 2,
+        out_shape=pltpu.VMEM((4, total), F32),
+        in_specs=[any_space] * 2 + [pl.BlockSpec(memory_space=pltpu.SMEM)] + [any_space] * 2,
         out_specs=vmem,
         scratch_shapes=[
             pltpu.VMEM((total, side, side), BF16),
-            pltpu.VMEM((side, 2 * side), BF16),
-            pltpu.VMEM((2 * side, 2 * side), BF16),
-            pltpu.VMEM((2 * side, 2 * side), BF16),
-            pltpu.VMEM((side, 2 * side), BF16),
+            pltpu.VMEM((6 * side, 2 * side), BF16),
             pltpu.VMEM((1, slots), jnp.int32),
             pltpu.SMEM((1, slots), jnp.int32),
             pltpu.VMEM((1, total), jnp.int32),
@@ -424,7 +483,7 @@
             pltpu.VMEM((2 * slots, side), F32),
             pltpu.VMEM((16, total), F32),
             pltpu.VMEM((2 * HALO + 1, 16, total), F32),
-            dma((8,)),
+            dma((5,)),
             dma,
             dma((2,)),
             dma((2 * chunks,)),
@@ -436,17 +495,18 @@
             collective_id=0, has_side_effects=True, vmem_limit_bytes=64_000_000
         ),
         name="exchange",
-    )(*dft_tables(side), pair_list, pair_count, tissue, patches)
+    )(dft_tables(side), pair_list, pair_count, tissue, patches)
     return pl.pallas_call(
-        relax,
+        unpack,
         out_shape=(
             jax.ShapeDtypeStruct((1, 2, slots), F32),
             jax.ShapeDtypeStruct((1, 2, total), F32),
         ),
         in_specs=[vmem],
         out_specs=(vmem, vmem),
-        name="relax",
-    )(halo)
+        compiler_params=pltpu.CompilerParams(vmem_limit_bytes=2_000_000),
+        name="unpack",
+    )(both)
 
 
 def solution(mesh):

time: 34.1 us -> 31.9 us (0.935)
  Pallas kernels: 32.6 us -> 30.5 us
    pallas_call x2, Pallas kernels: 32.6 us -> 30.5 us  [the longest x1 29.9 us: on_device(): pl.pallas_call(functools.partial(exchange, n), out_shape=pltpu.VMEM((4, t...]
where the time goes in v1:
time: 31.9 us; the launch traced here: 31.7 us
  Pallas kernels  30.5 us (96%)
  between operations  1.28 us (4%)
    pallas_call x1, Pallas kernels, on_device(): pl.pallas_call(functools.partial(exchange, n), out_shape=pltpu.VMEM((4, t...  29.9 us

profile of v1, /device:TPU:0, one launch (start us, length us, event | category | flops | bytes accessed | tf_op | source)
XLA Modules:
  0.0 31.7 jit_solution(8763344336750347840)
XLA Ops:
  1.3 29.9 %exchange.1.both = f32[4,128]{1,0:T(4,128)S(1)} custom-call(bf16[768,256]{1,0:T(8,128)(2,1)} %constant.2.clone.tables_any, s32[1,64]{1,0:T(1,128)} %list_any.1, s32[1]{0:T(128)S(6)} %copy.7.count_s, s32[1,128]{1,0:T(1,128)} %tissue_any.1, bf16[1,128,128,128]{3,2,1,0:T(8,128)(2,1)} %patches_any.1), custom_call_target="tpu_custom_call" | custom-call | tf_op jit(solution)/shard_map/exchange/pallas_call | solution.py:464
  31.2 0.6 %unpack.1 = (f32[1,2,64]{2,1,0:T(2,128)}, f32[1,2,128]{2,1,0:T(2,128)}) custom-call(f32[4,128]{1,0:T(4,128)S(1)} %exchange.1.both), custom_call_target="tpu_custom_call" | custom-call | tf_op jit(solution)/shard_map/unpack/pallas_call | solution.py:499

commit v2 on v1

--- a/solution.py
+++ b/solution.py
@@ -13,7 +13,7 @@
 STEP = 0.15
 CHUNK = 8
 PIECE = 2
-LOADS = 4
+BANDS = 2
 HALO = 3
 MESH = pl.DeviceIdType.MESH
 F32 = jnp.float32
@@ -83,7 +83,8 @@
     tissue_any,
     patches_any,
     out_ref,
-    patches,
+    patches_a,
+    patches_b,
     tables,
     list_v,
     list_s,
@@ -100,15 +101,17 @@
     packet,
     halo,
     load_sems,
-    smem_sem,
     list_sems,
     send_sems,
     recv_sems,
     halo_send,
     halo_recv,
+    near_sem,
+    far_sem,
 ):
     me = lax.axis_index("sec")
-    total, side, _ = patches.shape
+    patches = (patches_a, patches_b)
+    total, _, side = patches_a.shape
     slots = list_v.shape[1]
     chunks = slots // CHUNK
     offsets = [d for d in range(-HALO, HALO + 1) if d != 0]
@@ -119,7 +122,6 @@
             (
                 (list_any, list_s),
                 (list_any, list_v),
-                (patches_any.at[0], patches),
                 (tables_any, tables),
                 (tissue_any, tissue_v),
             )
@@ -127,22 +129,31 @@
     ]
     loads[0].start()
     loads[1].start()
-    part = total // LOADS
-    for i in range(LOADS):
-        rows = pl.ds(i * part, part)
-        pltpu.make_async_copy(patches_any.at[0, rows], patches.at[rows], load_sems.at[2]).start()
+    bands = [pl.ds(i * side // BANDS, side // BANDS) for i in range(BANDS)]
+    band_loads = [
+        pltpu.make_async_copy(
+            patches_any.at[0, :, band], patches[i], load_sems.at[4 + i]
+        )
+        for i, band in enumerate(bands)
+    ]
+    for load in band_loads:
+        load.start()
+    loads[2].start()
     loads[3].start()
-    loads[4].start()
 
     halo[...] = jnp.zeros_like(halo)
     far_note[...] = jnp.zeros_like(far_note)
 
     barrier = pltpu.get_barrier_semaphore()
-    for d in offsets:
-
-        @pl.when((me + d >= 0) & (me + d < n))
-        def _():
-            pl.semaphore_signal(barrier, inc=1, device_id={"sec": me + d}, device_id_type=MESH)
+
+    def greet(sem):
+        for to in (me + 1 - 2 * (me % 2), me - 1 + 2 * (me % 2)):
+
+            @pl.when((to >= 0) & (to < n))
+            def _():
+                pl.semaphore_signal(sem, inc=1, device_id={"sec": to}, device_id_type=MESH)
+
+    greet(barrier)
 
     peak_ref[...] = jnp.zeros_like(peak_ref)
     mass_ref[...] = jnp.ones_like(mass_ref)
@@ -159,7 +170,8 @@
     my_half = has_up * single(me)
     far_half = has_down * single(me - 1)
 
-    pl.semaphore_wait(barrier, jnp.minimum(me, HALO) + jnp.minimum(n - 1 - me, HALO))
+    sides = jnp.minimum(me, 1) + jnp.minimum(n - 1 - me, 1)
+    pl.semaphore_wait(barrier, sides)
 
     list_copy = pltpu.make_async_remote_copy(
         src_ref=note,
@@ -170,11 +182,20 @@
         device_id_type=MESH,
     )
 
+    slot_copy = pltpu.make_async_remote_copy(
+        src_ref=list_v,
+        dst_ref=far_s,
+        send_sem=list_sems.at[2],
+        recv_sem=list_sems.at[3],
+        device_id={"sec": me + 1},
+        device_id_type=MESH,
+    )
+
     @pl.when(me < n - 1)
     def _():
+        slot_copy.start()
         list_copy.start()
 
-    loads[2].wait()
 
     def patch_copy(q, to):
         return pltpu.make_async_remote_copy(
@@ -199,20 +220,38 @@
 
     def gather(source, q, c, first, count):
         for j in range(first, first + count):
-            outgoing[q * CHUNK + j] = patches[source[0, c * CHUNK + j]]
+            for part, band in zip(patches, bands):
+                outgoing[q * CHUNK + j, band] = part[source[0, c * CHUNK + j]]
 
     def send_up(c, carry):
         gather(list_s, c, c, 0, CHUNK)
         patch_copy(c, me + 1).start()
         return carry
 
-    lax.fori_loop(0, has_up * my_up, send_up, 0)
+    for i, band in enumerate(bands):
+        band_loads[i].wait()
+
+        @pl.when(has_up * my_up > 0)
+        def _():
+            for j in range(CHUNK):
+                outgoing[j, band] = patches[i][list_s[0, j]]
+            pltpu.make_async_remote_copy(
+                src_ref=outgoing.at[0:CHUNK, band],
+                dst_ref=incoming.at[0:CHUNK, band],
+                send_sem=send_sems.at[0],
+                recv_sem=recv_sems.at[0],
+                device_id={"sec": me + 1},
+                device_id_type=MESH,
+            ).start()
+
+    lax.fori_loop(1, has_up * my_up, send_up, 0)
 
     @pl.when(my_half > 0)
     def _():
         gather(list_s, my_up, my_up, 0, PIECE)
         piece_copy(my_up, 0, PIECE, me + 1).start()
 
+    greet(near_sem)
     right_ref = tables.at[0:side]
     left_ref = tables.at[side : 3 * side]
     inner_ref = tables.at[3 * side : 5 * side]
@@ -223,18 +262,21 @@
         for j in range(CHUNK):
             far = far_s[0, jnp.minimum(q, chunks - 1) * CHUNK + j]
             near = list_s[0, jnp.maximum(q - chunks, 0) * CHUNK + j]
-            images.append(patches[jnp.where(q < chunks, far, near)])
+            at = jnp.where(q < chunks, far, near)
+            images.append(jnp.concatenate([part[at] for part in patches], axis=0))
         for i, spec in enumerate(spectra(images, right_ref[...], left_ref[...])):
             own_spec[q * (CHUNK // 2) + i] = spec.astype(BF16)
         return carry
 
     @pl.when(me > 0)
     def _():
-        list_copy.wait_recv()
-
-    to_smem = pltpu.make_async_copy(far_note, far_s, smem_sem)
-    to_smem.start()
-    to_smem.wait()
+        slot_copy.wait_recv()
+
+    @pl.when(me == 0)
+    def _():
+        fill = pltpu.make_async_copy(list_v, far_s, list_sems.at[3])
+        fill.start()
+        fill.wait()
 
     @pl.when(far_half > 0)
     def _():
@@ -249,10 +291,16 @@
         return carry
 
     lax.fori_loop(down_from, down_from + has_down * (chunks - down_from), send_down, 0)
-    for load in loads[3:]:
+    for load in loads[2:]:
         load.wait()
     lax.fori_loop(chunks + my_up, chunks + my_up + has_up * (chunks - my_up), own_group, 0)
     lax.fori_loop(0, has_down * far_up + far_half, own_group, 0)
+
+    pl.semaphore_wait(near_sem, sides)
+    greet(far_sem)
+    @pl.when(me > 0)
+    def _():
+        list_copy.wait_recv()
 
     half = side // 2
     row = lax.broadcasted_iota(jnp.int32, (side, 1), 0)
@@ -356,6 +404,8 @@
     packet[4:5, 0 : 2 * slots] = flow_rows
     packet[5:6, 0 : 2 * slots] = flow_cols
 
+    pl.semaphore_wait(far_sem, sides)
+
     def halo_copy(d):
         return pltpu.make_async_remote_copy(
             src_ref=packet,
@@ -374,6 +424,7 @@
 
     @pl.when(me < n - 1)
     def _():
+        slot_copy.wait_send()
         list_copy.wait_send()
 
     def drain_up(c, carry):
@@ -467,14 +518,15 @@
         in_specs=[any_space] * 2 + [pl.BlockSpec(memory_space=pltpu.SMEM)] + [any_space] * 2,
         out_specs=vmem,
         scratch_shapes=[
-            pltpu.VMEM((total, side, side), BF16),
+            pltpu.VMEM((total, side // BANDS, side), BF16),
+            pltpu.VMEM((total, side // BANDS, side), BF16),
             pltpu.VMEM((6 * side, 2 * side), BF16),
             pltpu.VMEM((1, slots), jnp.int32),
             pltpu.SMEM((1, slots), jnp.int32),
             pltpu.VMEM((1, total), jnp.int32),
             pltpu.VMEM((2, slots), jnp.int32),
             pltpu.VMEM((2, slots), jnp.int32),
-            pltpu.SMEM((2, slots), jnp.int32),
+            pltpu.SMEM((1, slots), jnp.int32),
             pltpu.VMEM((2 * slots, side, side), BF16),
             pltpu.VMEM((2 * slots, side, side), BF16),
             pltpu.VMEM((slots, 2 * side, 2 * side), BF16),
@@ -483,13 +535,14 @@
             pltpu.VMEM((2 * slots, side), F32),
             pltpu.VMEM((16, total), F32),
             pltpu.VMEM((2 * HALO + 1, 16, total), F32),
-            dma((5,)),
-            dma,
-            dma((2,)),
+            dma((4 + BANDS,)),
+            dma((4,)),
             dma((2 * chunks,)),
             dma((2 * chunks,)),
             dma((2 * HALO + 1,)),
             dma((2 * HALO + 1,)),
+            pltpu.SemaphoreType.REGULAR,
+            pltpu.SemaphoreType.REGULAR,
         ],
         compiler_params=pltpu.CompilerParams(
             collective_id=0, has_side_effects=True, vmem_limit_bytes=64_000_000

time: 31.9 us -> 31.6 us (level)
  Pallas kernels: 30.5 us -> 30.1 us
    pallas_call x1, Pallas kernels: 29.9 us -> 29.5 us  [on_device(): pl.pallas_call(functools.partial(exchange, n), out_shape=pltpu.VMEM((4, t...]
where the time goes in v2:
time: 31.6 us; the launch traced here: 31.4 us
  Pallas kernels  30.1 us (95%)
  between operations  1.28 us (4%)
    pallas_call x1, Pallas kernels, on_device(): pl.pallas_call(functools.partial(exchange, n), out_shape=pltpu.VMEM((4, t...  29.5 us

profile of v2, /device:TPU:0, one launch (start us, length us, event | category | flops | bytes accessed | tf_op | source)
XLA Modules:
  0.0 31.4 jit_solution(15694242777080139878)
XLA Ops:
  1.3 29.5 %exchange.1.both = f32[4,128]{1,0:T(4,128)S(1)} custom-call(bf16[768,256]{1,0:T(8,128)(2,1)} %constant.2.clone.tables_any, s32[1,64]{1,0:T(1,128)} %list_any.1, s32[1]{0:T(128)S(6)} %copy.7.count_s, s32[1,128]{1,0:T(1,128)} %tissue_any.1, bf16[1,128,128,128]{3,2,1,0:T(8,128)(2,1)} %patches_any.1), custom_call_target="tpu_custom_call" | custom-call | tf_op jit(solution)/shard_map/exchange/pallas_call | solution.py:515
  30.8 0.6 %unpack.1 = (f32[1,2,64]{2,1,0:T(2,128)}, f32[1,2,128]{2,1,0:T(2,128)}) custom-call(f32[4,128]{1,0:T(4,128)S(1)} %exchange.1.both), custom_call_target="tpu_custom_call" | custom-call | tf_op jit(solution)/shard_map/unpack/pallas_call | solution.py:552

commit v3 on v2

--- a/solution.py
+++ b/solution.py
@@ -201,7 +201,7 @@
         return pltpu.make_async_remote_copy(
             src_ref=outgoing.at[pl.ds(q * CHUNK, CHUNK)],
             dst_ref=incoming.at[pl.ds(q * CHUNK, CHUNK)],
-            send_sem=send_sems.at[q],
+            send_sem=send_sems.at[0],
             recv_sem=recv_sems.at[q],
             device_id={"sec": to},
             device_id_type=MESH,
@@ -212,7 +212,7 @@
         return pltpu.make_async_remote_copy(
             src_ref=outgoing.at[at],
             dst_ref=incoming.at[at],
-            send_sem=send_sems.at[q],
+            send_sem=send_sems.at[0],
             recv_sem=recv_sems.at[q],
             device_id={"sec": to},
             device_id_type=MESH,
@@ -410,7 +410,7 @@
         return pltpu.make_async_remote_copy(
             src_ref=packet,
             dst_ref=halo.at[HALO - d],
-            send_sem=halo_send.at[HALO - d],
+            send_sem=halo_send.at[0],
             recv_sem=halo_recv.at[HALO - d],
             device_id={"sec": me + d},
             device_id_type=MESH,
@@ -537,9 +537,9 @@
             pltpu.VMEM((2 * HALO + 1, 16, total), F32),
             dma((4 + BANDS,)),
             dma((4,)),
+            dma((1,)),
             dma((2 * chunks,)),
-            dma((2 * chunks,)),
-            dma((2 * HALO + 1,)),
+            dma((1,)),
             dma((2 * HALO + 1,)),
             pltpu.SemaphoreType.REGULAR,
             pltpu.SemaphoreType.REGULAR,

time: 31.6 us -> 31.4 us (level)
  no operation moved by 1% of the time
where the time goes in v3:
time: 31.4 us; the launch traced here: 31.2 us
  Pallas kernels  29.9 us (95%)
  between operations  1.28 us (4%)
    pallas_call x1, Pallas kernels, on_device(): pl.pallas_call(functools.partial(exchange, n), out_shape=pltpu.VMEM((4, t...  29.4 us

profile of v3, /device:TPU:0, one launch (start us, length us, event | category | flops | bytes accessed | tf_op | source)
XLA Modules:
  0.0 31.2 jit_solution(5622252296399880992)
XLA Ops:
  1.3 29.4 %exchange.1.both = f32[4,128]{1,0:T(4,128)S(1)} custom-call(bf16[768,256]{1,0:T(8,128)(2,1)} %constant.2.clone.tables_any, s32[1,64]{1,0:T(1,128)} %list_any.1, s32[1]{0:T(128)S(6)} %copy.7.count_s, s32[1,128]{1,0:T(1,128)} %tissue_any.1, bf16[1,128,128,128]{3,2,1,0:T(8,128)(2,1)} %patches_any.1), custom_call_target="tpu_custom_call" | custom-call | tf_op jit(solution)/shard_map/exchange/pallas_call | solution.py:515
  30.6 0.6 %unpack.1 = (f32[1,2,64]{2,1,0:T(2,128)}, f32[1,2,128]{2,1,0:T(2,128)}) custom-call(f32[4,128]{1,0:T(4,128)S(1)} %exchange.1.both), custom_call_target="tpu_custom_call" | custom-call | tf_op jit(solution)/shard_map/unpack/pallas_call | solution.py:552

commit v4 on v3

--- a/solution.py
+++ b/solution.py
@@ -13,6 +13,7 @@
 STEP = 0.15
 CHUNK = 8
 PIECE = 2
+HALF = CHUNK // 2
 BANDS = 2
 HALO = 3
 MESH = pl.DeviceIdType.MESH
@@ -167,6 +168,8 @@
     has_down = jnp.minimum(me, 1)
     my_up = up_chunks(me, n, chunks)
     far_up = up_chunks(me - 1, n, chunks)
+    tail_near = has_up * (me % 2) * jnp.minimum(chunks - 1 - my_up, 1)
+    tail_far = has_down * (1 - me % 2) * jnp.minimum(chunks - 1 - far_up, 1)
     my_half = has_up * single(me)
     far_half = has_down * single(me - 1)
 
@@ -203,6 +206,17 @@
             dst_ref=incoming.at[pl.ds(q * CHUNK, CHUNK)],
             send_sem=send_sems.at[0],
             recv_sem=recv_sems.at[q],
+            device_id={"sec": to},
+            device_id_type=MESH,
+        )
+
+    def half_copy(i, to):
+        at = pl.ds(2 * slots - CHUNK + i * HALF, HALF)
+        return pltpu.make_async_remote_copy(
+            src_ref=outgoing.at[at],
+            dst_ref=incoming.at[at],
+            send_sem=send_sems.at[0],
+            recv_sem=recv_sems.at[2 * chunks - 1 + i],
             device_id={"sec": to},
             device_id_type=MESH,
         )
@@ -290,7 +304,15 @@
         patch_copy(chunks + c, me - 1).start()
         return carry
 
-    lax.fori_loop(down_from, down_from + has_down * (chunks - down_from), send_down, 0)
+    n_down = has_down * (chunks - down_from) - tail_far
+    lax.fori_loop(down_from, down_from + n_down, send_down, 0)
+
+    @pl.when(tail_far > 0)
+    def _():
+        for i in range(2):
+            gather(far_s, 2 * chunks - 1, chunks - 1, i * HALF, HALF)
+            half_copy(i, me - 1).start()
+
     for load in loads[2:]:
         load.wait()
     lax.fori_loop(chunks + my_up, chunks + my_up + has_up * (chunks - my_up), own_group, 0)
@@ -307,31 +329,14 @@
     row_lag = ((row + half) % side - half).astype(F32)
     scale = 64.0 / float(side * side * side * side)
 
-    def match_group(t, carry):
-        start_a, count_a, start_b = carry
-        q = jnp.where(t < count_a, start_a + t, start_b + t - count_a)
-        is_far_half = (q == far_up) & (far_half > 0)
-        is_my_half = (q == chunks + my_up) & (my_half > 0)
-
-        @pl.when(is_far_half)
-        def _():
-            piece_copy(q, 0, PIECE, me).wait_recv()
-
-        @pl.when(is_my_half)
-        def _():
-            piece_copy(q, PIECE, CHUNK - PIECE, me).wait_recv()
-
-        @pl.when(jnp.logical_not(is_far_half | is_my_half))
-        def _():
-            patch_copy(q, me).wait_recv()
-
-        sign = jnp.where(q < chunks, -1.0, 1.0).astype(F32)
-        images = [incoming[q * CHUNK + j] for j in range(CHUNK)]
+    def match(slot, size):
+        sign = jnp.where(slot < slots, -1.0, 1.0).astype(F32)
+        images = [incoming[slot + j] for j in range(size)]
         crosses = []
         for i, spec in enumerate(spectra(images, right_ref[...], left_ref[...])):
             ar = spec[:side].astype(BF16).astype(F32)
             ai = spec[side:].astype(BF16).astype(F32)
-            own = own_spec[q * (CHUNK // 2) + i].astype(F32)
+            own = own_spec[slot // 2 + i].astype(F32)
             br, bi = own[:side], own[side:]
             cr = (br * ar + bi * ai).astype(BF16)
             ci = ((br * ai - bi * ar) * sign).astype(BF16)
@@ -339,7 +344,7 @@
             crosses.append(jnp.concatenate([cr[:, side:], ci[:, side:]], axis=1))
         inner = dot(jnp.concatenate(crosses, axis=0), inner_ref[...]).astype(BF16)
         peaks, masses, moments = [], [], []
-        for i in range(CHUNK // 2):
+        for i in range(size // 2):
             scores = dot(last_ref[...], stacked(inner, 2 * i, 2 * i + 1, side)) * scale
             peak = jnp.max(scores, axis=0, keepdims=True)
             e = jnp.exp(scores - peak)
@@ -348,10 +353,25 @@
             for parts, value in ((peaks, peak), (masses, mass), (moments, moment)):
                 parts.append(value[:, :side])
                 parts.append(value[:, side:])
-        at = pl.ds(pl.multiple_of(q * CHUNK, CHUNK), CHUNK)
+        at = pl.ds(slot, size)
         peak_ref[at, :] = jnp.concatenate(peaks, axis=0)
         mass_ref[at, :] = jnp.concatenate(masses, axis=0)
         moment_ref[at, :] = jnp.concatenate(moments, axis=0)
+
+    def match_group(t, carry):
+        start_a, count_a, start_b = carry
+        q = jnp.where(t < count_a, start_a + t, start_b + t - count_a)
+        is_my_half = (q == chunks + my_up) & (my_half > 0)
+
+        @pl.when(is_my_half)
+        def _():
+            piece_copy(q, PIECE, CHUNK - PIECE, me).wait_recv()
+
+        @pl.when(jnp.logical_not(is_my_half))
+        def _():
+            patch_copy(q, me).wait_recv()
+
+        match(pl.multiple_of(q * CHUNK, CHUNK), CHUNK)
         return carry
 
     n_far = has_down * far_up + far_half
@@ -360,7 +380,25 @@
     start_a = (1 - odd) * (chunks + my_up)
     start_b = odd * (chunks + my_up)
     count_a = odd * n_far + (1 - odd) * n_near
-    lax.fori_loop(0, n_far + n_near, match_group, (start_a, count_a, start_b))
+    n_main = n_far + n_near - far_half - tail_near
+    lax.fori_loop(0, n_main, match_group, (start_a, count_a, start_b))
+
+    def match_tail(i, carry):
+        @pl.when(far_half > 0)
+        def _():
+            piece_copy(far_up, 0, PIECE, me).wait_recv()
+
+        for k in range(2):
+
+            @pl.when((tail_near > 0) & (i == k))
+            def _():
+                half_copy(k, me).wait_recv()
+
+        near_slot = 2 * slots - CHUNK + i * HALF
+        match(pl.multiple_of(jnp.where(far_half > 0, far_up * CHUNK, near_slot), HALF), HALF)
+        return carry
+
+    lax.fori_loop(0, far_half + 2 * tail_near, match_tail, 0)
 
     peak = peak_ref[...]
     weight = jnp.exp(peak - jnp.max(peak, axis=1, keepdims=True))
@@ -441,7 +479,12 @@
         patch_copy(chunks + c, me - 1).wait_send()
         return carry
 
-    lax.fori_loop(down_from, down_from + has_down * (chunks - down_from), drain_down, 0)
+    lax.fori_loop(down_from, down_from + n_down, drain_down, 0)
+
+    @pl.when(tail_far > 0)
+    def _():
+        for i in range(2):
+            half_copy(i, me - 1).wait_send()
 
     @pl.when(far_half > 0)
     def _():
@@ -538,7 +581,7 @@
             dma((4 + BANDS,)),
             dma((4,)),
             dma((1,)),
-            dma((2 * chunks,)),
+            dma((2 * chunks + 1,)),
             dma((1,)),
             dma((2 * HALO + 1,)),
             pltpu.SemaphoreType.REGULAR,

time: 31.4 us -> 31.2 us (level)
  no operation moved by 1% of the time
where the time goes in v4:
time: 31.2 us; the launch traced here: 31.1 us
  Pallas kernels  29.8 us (96%)
  between operations  1.28 us (4%)
    pallas_call x1, Pallas kernels, on_device(): pl.pallas_call(functools.partial(exchange, n), out_shape=pltpu.VMEM((4, t...  29.2 us

profile of v4, /device:TPU:0, one launch (start us, length us, event | category | flops | bytes accessed | tf_op | source)
XLA Modules:
  0.0 31.1 jit_solution(17855241954038969364)
XLA Ops:
  1.3 29.2 %exchange.1.both = f32[4,128]{1,0:T(4,128)S(1)} custom-call(bf16[768,256]{1,0:T(8,128)(2,1)} %constant.2.clone.tables_any, s32[1,64]{1,0:T(1,128)} %list_any.1, s32[1]{0:T(128)S(6)} %copy.7.count_s, s32[1,128]{1,0:T(1,128)} %tissue_any.1, bf16[1,128,128,128]{3,2,1,0:T(8,128)(2,1)} %patches_any.1), custom_call_target="tpu_custom_call" | custom-call | tf_op jit(solution)/shard_map/exchange/pallas_call | solution.py:558
  30.5 0.6 %unpack.1 = (f32[1,2,64]{2,1,0:T(2,128)}, f32[1,2,128]{2,1,0:T(2,128)}) custom-call(f32[4,128]{1,0:T(4,128)S(1)} %exchange.1.both), custom_call_target="tpu_custom_call" | custom-call | tf_op jit(solution)/shard_map/unpack/pallas_call | solution.py:595

commit v5 on v4

--- a/solution.py
+++ b/solution.py
@@ -70,6 +70,14 @@
 
 def single(pair):
     return pair % 2
+
+
+def up_tail(up):
+    return jnp.minimum(jnp.maximum(up - 1, 0), 1)
+
+
+def down_tail(up, chunks):
+    return jnp.minimum(chunks - 1 - up, 1)
 
 
 def up_chunks(pair, n, chunks):
@@ -168,8 +176,10 @@
     has_down = jnp.minimum(me, 1)
     my_up = up_chunks(me, n, chunks)
     far_up = up_chunks(me - 1, n, chunks)
-    tail_near = has_up * (me % 2) * jnp.minimum(chunks - 1 - my_up, 1)
-    tail_far = has_down * (1 - me % 2) * jnp.minimum(chunks - 1 - far_up, 1)
+    my_odd, far_odd = has_up * (me % 2), has_down * (1 - me % 2)
+    up_tail_to, up_tail_in = my_odd * up_tail(my_up), far_odd * up_tail(far_up)
+    down_tail_in, down_tail_to = my_odd * down_tail(my_up, chunks), far_odd * down_tail(far_up, chunks)
+    tail_in = up_tail_in + down_tail_in
     my_half = has_up * single(me)
     far_half = has_down * single(me - 1)
 
@@ -210,13 +220,13 @@
             device_id_type=MESH,
         )
 
-    def half_copy(i, to):
-        at = pl.ds(2 * slots - CHUNK + i * HALF, HALF)
+    def half_copy(q, i, to):
+        at = pl.ds(q * CHUNK + i * HALF, HALF)
         return pltpu.make_async_remote_copy(
             src_ref=outgoing.at[at],
             dst_ref=incoming.at[at],
             send_sem=send_sems.at[0],
-            recv_sem=recv_sems.at[2 * chunks - 1 + i],
+            recv_sem=recv_sems.at[2 * chunks + i],
             device_id={"sec": to},
             device_id_type=MESH,
         )
@@ -258,12 +268,19 @@
                 device_id_type=MESH,
             ).start()
 
-    lax.fori_loop(1, has_up * my_up, send_up, 0)
+    n_up = has_up * my_up - up_tail_to
+    lax.fori_loop(1, n_up, send_up, 0)
 
     @pl.when(my_half > 0)
     def _():
         gather(list_s, my_up, my_up, 0, PIECE)
         piece_copy(my_up, 0, PIECE, me + 1).start()
+
+    @pl.when(up_tail_to > 0)
+    def _():
+        for i in range(2):
+            gather(list_s, my_up - 1, my_up - 1, i * HALF, HALF)
+            half_copy(my_up - 1, i, me + 1).start()
 
     greet(near_sem)
     right_ref = tables.at[0:side]
@@ -304,14 +321,14 @@
         patch_copy(chunks + c, me - 1).start()
         return carry
 
-    n_down = has_down * (chunks - down_from) - tail_far
+    n_down = has_down * (chunks - down_from) - down_tail_to
     lax.fori_loop(down_from, down_from + n_down, send_down, 0)
 
-    @pl.when(tail_far > 0)
+    @pl.when(down_tail_to > 0)
     def _():
         for i in range(2):
             gather(far_s, 2 * chunks - 1, chunks - 1, i * HALF, HALF)
-            half_copy(i, me - 1).start()
+            half_copy(2 * chunks - 1, i, me - 1).start()
 
     for load in loads[2:]:
         load.wait()
@@ -353,25 +370,34 @@
             for parts, value in ((peaks, peak), (masses, mass), (moments, moment)):
                 parts.append(value[:, :side])
                 parts.append(value[:, side:])
-        at = pl.ds(slot, size)
-        peak_ref[at, :] = jnp.concatenate(peaks, axis=0)
-        mass_ref[at, :] = jnp.concatenate(masses, axis=0)
-        moment_ref[at, :] = jnp.concatenate(moments, axis=0)
+        return [jnp.concatenate(parts, axis=0) for parts in (peaks, masses, moments)]
 
     def match_group(t, carry):
         start_a, count_a, start_b = carry
         q = jnp.where(t < count_a, start_a + t, start_b + t - count_a)
+        skip = up_tail_in * (q < chunks).astype(jnp.int32) * (q >= far_up - 1).astype(jnp.int32)
+        q = q + skip
+        is_far_half = (q == far_up) & (far_half > 0)
         is_my_half = (q == chunks + my_up) & (my_half > 0)
+
+        @pl.when(is_far_half)
+        def _():
+            piece_copy(q, 0, PIECE, me).wait_recv()
 
         @pl.when(is_my_half)
         def _():
             piece_copy(q, PIECE, CHUNK - PIECE, me).wait_recv()
 
-        @pl.when(jnp.logical_not(is_my_half))
+        @pl.when(jnp.logical_not(is_far_half | is_my_half))
         def _():
             patch_copy(q, me).wait_recv()
 
-        match(pl.multiple_of(q * CHUNK, CHUNK), CHUNK)
+        slot = pl.multiple_of(q * CHUNK, CHUNK)
+        peaks, masses, moments = match(slot, CHUNK)
+        at = pl.ds(slot, CHUNK)
+        peak_ref[at, :] = peaks
+        mass_ref[at, :] = masses
+        moment_ref[at, :] = moments
         return carry
 
     n_far = has_down * far_up + far_half
@@ -380,25 +406,9 @@
     start_a = (1 - odd) * (chunks + my_up)
     start_b = odd * (chunks + my_up)
     count_a = odd * n_far + (1 - odd) * n_near
-    n_main = n_far + n_near - far_half - tail_near
+    tail_q = jnp.where(up_tail_in > 0, far_up - 1, 2 * chunks - 1)
+    n_main = n_far + n_near - tail_in
     lax.fori_loop(0, n_main, match_group, (start_a, count_a, start_b))
-
-    def match_tail(i, carry):
-        @pl.when(far_half > 0)
-        def _():
-            piece_copy(far_up, 0, PIECE, me).wait_recv()
-
-        for k in range(2):
-
-            @pl.when((tail_near > 0) & (i == k))
-            def _():
-                half_copy(k, me).wait_recv()
-
-        near_slot = 2 * slots - CHUNK + i * HALF
-        match(pl.multiple_of(jnp.where(far_half > 0, far_up * CHUNK, near_slot), HALF), HALF)
-        return carry
-
-    lax.fori_loop(0, far_half + 2 * tail_near, match_tail, 0)
 
     peak = peak_ref[...]
     weight = jnp.exp(peak - jnp.max(peak, axis=1, keepdims=True))
@@ -422,7 +432,8 @@
     slot = jnp.where(is_far, place, place - slots)
     first = jnp.where(is_far, 0, (chunks - n_near) * CHUNK + my_half * PIECE)
     stop = jnp.minimum(jnp.where(is_far, n_far * CHUNK - far_half * (CHUNK - PIECE), slots), counts)
-    live = (slot >= first) & (slot < stop)
+    late = (place >= tail_q * CHUNK) & (place < tail_q * CHUNK + CHUNK) & (tail_in > 0)
+    live = (slot >= first) & (slot < stop) & jnp.logical_not(late)
     flow_rows = jnp.where(live, rows_num[0:1] / mass_all, 0.0)
     flow_cols = jnp.where(live, sums[1:2] / mass_all, 0.0)
     which = lax.broadcasted_iota(jnp.int32, (total, 2 * slots), 0)
@@ -442,6 +453,52 @@
     packet[4:5, 0 : 2 * slots] = flow_rows
     packet[5:6, 0 : 2 * slots] = flow_cols
 
+    lane = lax.broadcasted_iota(jnp.int32, (HALF, side), 1)
+    step = lax.broadcasted_iota(jnp.int32, (HALF, side), 0)
+    late_lag = ((lane + half) % side - half).astype(F32)
+    spot = lax.broadcasted_iota(jnp.int32, (HALF, total), 1)
+    turn = lax.broadcasted_iota(jnp.int32, (HALF, total), 0)
+    late_far = up_tail_in > 0
+    late_count = jnp.where(late_far, far_note[1:2, 0:1], jnp.full((1, 1), count, jnp.int32))
+
+    def match_tail(i, carry):
+        for k in range(2):
+
+            @pl.when(i == k)
+            def _():
+                half_copy(tail_q, k, me).wait_recv()
+
+        at = pl.multiple_of(tail_q * CHUNK + i * HALF, HALF)
+        peak, mass, moment = match(at, HALF)
+        weight = jnp.exp(peak - jnp.max(peak, axis=1, keepdims=True))
+        mass = mass * weight
+        whole = jnp.sum(mass, axis=1, keepdims=True)
+        rows = jnp.sum(moment * weight, axis=1, keepdims=True) / whole
+        cols = jnp.sum(mass * late_lag, axis=1, keepdims=True) / whole
+        own_at = jnp.where(late_far, at, at - slots)
+        ids = jnp.zeros((HALF, total), jnp.int32)
+        for j in range(HALF):
+            listed = jnp.where(late_far, far_s[0, own_at + j], list_s[0, own_at + j])
+            ids = jnp.where(turn == j, listed, ids)
+        alive = turn + own_at < late_count
+        hit = (spot == ids) & alive
+        here = (spot == turn + at) & alive
+        picks = [
+            jnp.where(hit, rows, 0.0),
+            jnp.where(hit, cols, 0.0),
+            hit.astype(F32),
+            jnp.where(here, rows, 0.0),
+            jnp.where(here, cols, 0.0),
+        ]
+        picks = [jnp.sum(pick, axis=0, keepdims=True) for pick in picks]
+        extra = jnp.concatenate(picks[:3], axis=0)
+        packet[0:3] = packet[0:3] + jnp.where(late_far, extra, 0.0)
+        packet[8:11] = packet[8:11] + jnp.where(late_far, 0.0, extra)
+        packet[4:6] = packet[4:6] + jnp.concatenate(picks[3:], axis=0)
+        return carry
+
+    lax.fori_loop(0, 2 * tail_in, match_tail, 0)
+
     pl.semaphore_wait(far_sem, sides)
 
     def halo_copy(d):
@@ -469,7 +526,12 @@
         patch_copy(c, me + 1).wait_send()
         return carry
 
-    lax.fori_loop(0, has_up * my_up, drain_up, 0)
+    lax.fori_loop(0, n_up, drain_up, 0)
+
+    @pl.when(up_tail_to > 0)
+    def _():
+        for i in range(2):
+            half_copy(my_up - 1, i, me + 1).wait_send()
 
     @pl.when(my_half > 0)
     def _():
@@ -481,10 +543,10 @@
 
     lax.fori_loop(down_from, down_from + n_down, drain_down, 0)
 
-    @pl.when(tail_far > 0)
+    @pl.when(down_tail_to > 0)
     def _():
         for i in range(2):
-            half_copy(i, me - 1).wait_send()
+            half_copy(2 * chunks - 1, i, me - 1).wait_send()
 
     @pl.when(far_half > 0)
     def _():
@@ -581,7 +643,7 @@
             dma((4 + BANDS,)),
             dma((4,)),
             dma((1,)),
-            dma((2 * chunks + 1,)),
+            dma((2 * chunks + 2,)),
             dma((1,)),
             dma((2 * HALO + 1,)),
             pltpu.SemaphoreType.REGULAR,

time: 31.2 us -> 31 us (level)
  no operation moved by 1% of the time
where the time goes in v5:
time: 31 us; the launch traced here: 30.8 us
  Pallas kernels  29.5 us (95%)
  between operations  1.28 us (4%)
    pallas_call x1, Pallas kernels, on_device(): pl.pallas_call(functools.partial(exchange, n), out_shape=pltpu.VMEM((4, t...  29 us

profile of v5, /device:TPU:0, one launch (start us, length us, event | category | flops | bytes accessed | tf_op | source)
XLA Modules:
  0.0 30.8 jit_solution(10576234918120892636)
XLA Ops:
  1.3 29.0 %exchange.1.both = f32[4,128]{1,0:T(4,128)S(1)} custom-call(bf16[768,256]{1,0:T(8,128)(2,1)} %constant.2.clone.tables_any, s32[1,64]{1,0:T(1,128)} %list_any.1, s32[1]{0:T(128)S(6)} %copy.7.count_s, s32[1,128]{1,0:T(1,128)} %tissue_any.1, bf16[1,128,128,128]{3,2,1,0:T(8,128)(2,1)} %patches_any.1), custom_call_target="tpu_custom_call" | custom-call | tf_op jit(solution)/shard_map/exchange/pallas_call | solution.py:620
  30.2 0.6 %unpack.1 = (f32[1,2,64]{2,1,0:T(2,128)}, f32[1,2,128]{2,1,0:T(2,128)}) custom-call(f32[4,128]{1,0:T(4,128)S(1)} %exchange.1.both), custom_call_target="tpu_custom_call" | custom-call | tf_op jit(solution)/shard_map/unpack/pallas_call | solution.py:657

commit v6 on v5

--- a/solution.py
+++ b/solution.py
@@ -12,7 +12,7 @@
 SPRING = 0.25
 STEP = 0.15
 CHUNK = 8
-PIECE = 2
+PIECES = (1, 2, 3)
 HALF = CHUNK // 2
 BANDS = 2
 HALO = 3
@@ -68,8 +68,10 @@
     return pltpu.roll(x, shift % x.shape[-1], x.ndim - 1)
 
 
-def single(pair):
-    return pair % 2
+def piece_of(pair, n):
+    spot, middle = (pair + 1) // 2, n // 4
+    size = 1 + jnp.minimum(jnp.maximum(middle + 1 - spot, 0), 2)
+    return (pair % 2) * size
 
 
 def up_tail(up):
@@ -180,8 +182,9 @@
     up_tail_to, up_tail_in = my_odd * up_tail(my_up), far_odd * up_tail(far_up)
     down_tail_in, down_tail_to = my_odd * down_tail(my_up, chunks), far_odd * down_tail(far_up, chunks)
     tail_in = up_tail_in + down_tail_in
-    my_half = has_up * single(me)
-    far_half = has_down * single(me - 1)
+    my_piece = has_up * piece_of(me, n)
+    far_piece = has_down * piece_of(me - 1, n)
+    my_half, far_half = jnp.minimum(my_piece, 1), jnp.minimum(far_piece, 1)
 
     sides = jnp.minimum(me, 1) + jnp.minimum(n - 1 - me, 1)
     pl.semaphore_wait(barrier, sides)
@@ -271,10 +274,12 @@
     n_up = has_up * my_up - up_tail_to
     lax.fori_loop(1, n_up, send_up, 0)
 
-    @pl.when(my_half > 0)
-    def _():
-        gather(list_s, my_up, my_up, 0, PIECE)
-        piece_copy(my_up, 0, PIECE, me + 1).start()
+    for size in PIECES:
+
+        @pl.when(my_piece == size)
+        def _():
+            gather(list_s, my_up, my_up, 0, size)
+            piece_copy(my_up, 0, size, me + 1).start()
 
     @pl.when(up_tail_to > 0)
     def _():
@@ -309,10 +314,12 @@
         fill.start()
         fill.wait()
 
-    @pl.when(far_half > 0)
-    def _():
-        gather(far_s, chunks + far_up, far_up, PIECE, CHUNK - PIECE)
-        piece_copy(chunks + far_up, PIECE, CHUNK - PIECE, me - 1).start()
+    for size in PIECES:
+
+        @pl.when(far_piece == size)
+        def _():
+            gather(far_s, chunks + far_up, far_up, size, CHUNK - size)
+            piece_copy(chunks + far_up, size, CHUNK - size, me - 1).start()
 
     down_from = far_up + far_half
 
@@ -380,13 +387,15 @@
         is_far_half = (q == far_up) & (far_half > 0)
         is_my_half = (q == chunks + my_up) & (my_half > 0)
 
-        @pl.when(is_far_half)
-        def _():
-            piece_copy(q, 0, PIECE, me).wait_recv()
-
-        @pl.when(is_my_half)
-        def _():
-            piece_copy(q, PIECE, CHUNK - PIECE, me).wait_recv()
+        for size in PIECES:
+
+            @pl.when(is_far_half & (far_piece == size))
+            def _():
+                piece_copy(q, 0, size, me).wait_recv()
+
+            @pl.when(is_my_half & (my_piece == size))
+            def _():
+                piece_copy(q, size, CHUNK - size, me).wait_recv()
 
         @pl.when(jnp.logical_not(is_far_half | is_my_half))
         def _():
@@ -430,8 +439,8 @@
     counts = jnp.concatenate([far[1:2], jnp.full((1, slots), count, jnp.int32)], axis=1)
     lists = jnp.concatenate([far[0:1], list_v[...]], axis=1)
     slot = jnp.where(is_far, place, place - slots)
-    first = jnp.where(is_far, 0, (chunks - n_near) * CHUNK + my_half * PIECE)
-    stop = jnp.minimum(jnp.where(is_far, n_far * CHUNK - far_half * (CHUNK - PIECE), slots), counts)
+    first = jnp.where(is_far, 0, (chunks - n_near) * CHUNK + my_piece)
+    stop = jnp.minimum(jnp.where(is_far, n_far * CHUNK - (CHUNK * far_half - far_piece), slots), counts)
     late = (place >= tail_q * CHUNK) & (place < tail_q * CHUNK + CHUNK) & (tail_in > 0)
     live = (slot >= first) & (slot < stop) & jnp.logical_not(late)
     flow_rows = jnp.where(live, rows_num[0:1] / mass_all, 0.0)
@@ -533,9 +542,11 @@
         for i in range(2):
             half_copy(my_up - 1, i, me + 1).wait_send()
 
-    @pl.when(my_half > 0)
-    def _():
-        piece_copy(my_up, 0, PIECE, me + 1).wait_send()
+    for size in PIECES:
+
+        @pl.when(my_piece == size)
+        def _():
+            piece_copy(my_up, 0, size, me + 1).wait_send()
 
     def drain_down(c, carry):
         patch_copy(chunks + c, me - 1).wait_send()
@@ -548,9 +559,11 @@
         for i in range(2):
             half_copy(2 * chunks - 1, i, me - 1).wait_send()
 
-    @pl.when(far_half > 0)
-    def _():
-        piece_copy(chunks + far_up, PIECE, CHUNK - PIECE, me - 1).wait_send()
+    for size in PIECES:
+
+        @pl.when(far_piece == size)
+        def _():
+            piece_copy(chunks + far_up, size, CHUNK - size, me - 1).wait_send()
 
     for d in offsets:
 

time: 31 us -> 30.7 us (level)
    pallas_call x1, Pallas kernels: 29 us -> 28.6 us  [on_device(): pl.pallas_call(functools.partial(exchange, n), out_shape=pltpu.VMEM((4, t...]
where the time goes in v6:
time: 30.7 us; the launch traced here: 30.5 us
  Pallas kernels  29.2 us (95%)
  between operations  1.28 us (4%)
    pallas_call x1, Pallas kernels, on_device(): pl.pallas_call(functools.partial(exchange, n), out_shape=pltpu.VMEM((4, t...  28.6 us

profile of v6, /device:TPU:0, one launch (start us, length us, event | category | flops | bytes accessed | tf_op | source)
XLA Modules:
  0.0 30.5 jit_solution(18177258922820240640)
XLA Ops:
  1.3 28.6 %exchange.1.both = f32[4,128]{1,0:T(4,128)S(1)} custom-call(bf16[768,256]{1,0:T(8,128)(2,1)} %constant.2.clone.tables_any, s32[1,64]{1,0:T(1,128)} %list_any.1, s32[1]{0:T(128)S(6)} %copy.7.count_s, s32[1,128]{1,0:T(1,128)} %tissue_any.1, bf16[1,128,128,128]{3,2,1,0:T(8,128)(2,1)} %patches_any.1), custom_call_target="tpu_custom_call" | custom-call | tf_op jit(solution)/shard_map/exchange/pallas_call | solution.py:633
  29.9 0.6 %unpack.1 = (f32[1,2,64]{2,1,0:T(2,128)}, f32[1,2,128]{2,1,0:T(2,128)}) custom-call(f32[4,128]{1,0:T(4,128)S(1)} %exchange.1.both), custom_call_target="tpu_custom_call" | custom-call | tf_op jit(solution)/shard_map/unpack/pallas_call | solution.py:670

commit v7 on v6

--- a/solution.py
+++ b/solution.py
@@ -500,22 +500,22 @@
             jnp.where(here, cols, 0.0),
         ]
         picks = [jnp.sum(pick, axis=0, keepdims=True) for pick in picks]
-        extra = jnp.concatenate(picks[:3], axis=0)
-        packet[0:3] = packet[0:3] + jnp.where(late_far, extra, 0.0)
-        packet[8:11] = packet[8:11] + jnp.where(late_far, 0.0, extra)
-        packet[4:6] = packet[4:6] + jnp.concatenate(picks[3:], axis=0)
+        blank = jnp.zeros((1, total), F32)
+        field = jnp.concatenate(picks[:3] + [blank] * 5, axis=0)
+        flows = jnp.concatenate([blank] * 4 + picks[3:] + [blank] * 2, axis=0)
+        packet[0:8] = packet[0:8] + (jnp.where(late_far, field, 0.0) + flows)
+        packet[8:16] = packet[8:16] + jnp.where(late_far, 0.0, field)
         return carry
 
+    pl.semaphore_wait(far_sem, sides)
     lax.fori_loop(0, 2 * tail_in, match_tail, 0)
-
-    pl.semaphore_wait(far_sem, sides)
 
     def halo_copy(d):
         return pltpu.make_async_remote_copy(
             src_ref=packet,
             dst_ref=halo.at[HALO - d],
             send_sem=halo_send.at[0],
-            recv_sem=halo_recv.at[HALO - d],
+            recv_sem=halo_recv.at[(HALO - d) - (d < 0)],
             device_id={"sec": me + d},
             device_id_type=MESH,
         )
@@ -658,7 +658,7 @@
             dma((1,)),
             dma((2 * chunks + 2,)),
             dma((1,)),
-            dma((2 * HALO + 1,)),
+            dma((2 * HALO,)),
             pltpu.SemaphoreType.REGULAR,
             pltpu.SemaphoreType.REGULAR,
         ],

time: 30.7 us -> 30.7 us (level)
  no operation moved by 1% of the time
where the time goes in v7:
time: 30.7 us; the launch traced here: 30.5 us
  Pallas kernels  29.2 us (95%)
  between operations  1.28 us (4%)
    pallas_call x1, Pallas kernels, on_device(): pl.pallas_call(functools.partial(exchange, n), out_shape=pltpu.VMEM((4, t...  28.6 us

profile of v7, /device:TPU:0, one launch (start us, length us, event | category | flops | bytes accessed | tf_op | source)
XLA Modules:
  0.0 30.5 jit_solution(11889931867439129734)
XLA Ops:
  1.3 28.6 %exchange.1.both = f32[4,128]{1,0:T(4,128)S(1)} custom-call(bf16[768,256]{1,0:T(8,128)(2,1)} %constant.2.clone.tables_any, s32[1,64]{1,0:T(1,128)} %list_any.1, s32[1]{0:T(128)S(6)} %copy.7.count_s, s32[1,128]{1,0:T(1,128)} %tissue_any.1, bf16[1,128,128,128]{3,2,1,0:T(8,128)(2,1)} %patches_any.1), custom_call_target="tpu_custom_call" | custom-call | tf_op jit(solution)/shard_map/exchange/pallas_call | solution.py:633
  29.9 0.6 %unpack.1 = (f32[1,2,64]{2,1,0:T(2,128)}, f32[1,2,128]{2,1,0:T(2,128)}) custom-call(f32[4,128]{1,0:T(4,128)S(1)} %exchange.1.both), custom_call_target="tpu_custom_call" | custom-call | tf_op jit(solution)/shard_map/unpack/pallas_call | solution.py:670
